TPU v7x, 32 devices: a whole 2x2x4 slice. The times are simulated.
32 devices in a mesh: dp: 8 (over z, y), tensor: 4 (over x, core).
Axes of the slice: x: 2, y: 2, z: 4, core: 2. Of those that a mesh axis runs over, the one named last changes fastest.
Arguments:
- tokens: bfloat16 [18688, 1024], P(('dp', 'tensor')), may hold values from -6 to 6
- cotangent: bfloat16 [18688, 1024], P(('dp', 'tensor')), may hold values from -6 to 6
- image_mask: int32 [32], P('dp'), may hold values 0 or 1
- norm_gains: bfloat16 [2, 1024], P(None, 'dp'), may hold values from 0.25 to 1.75
- norm_shifts: bfloat16 [4, 1024], P(None, 'dp'), may hold values from -1.796875 to 1.796875
- w_qkv: bfloat16 [3, 1024, 1024], P(None, 'dp', 'tensor'), may hold values from -0.25 to 0.25
- b_qv: bfloat16 [2, 1024], P(None, ('tensor', 'dp')), may hold values from -3 to 3
- w_out: bfloat16 [1024, 1024], P('tensor', 'dp'), may hold values from -0.4375 to 0.4375
- w_up: bfloat16 [1024, 4096], P('dp', 'tensor'), may hold values from -0.1875 to 0.1875
- up_bias: bfloat16 [4096], P(('tensor', 'dp')), may hold values from -3 to 3
- w_down: bfloat16 [4096, 1024], P('tensor', 'dp'), may hold values from -0.125 to 0.125
Outputs:
- layer_out: bfloat16 [18688, 1024], P(('dp', 'tensor'))
- grad_tokens: bfloat16 [18688, 1024], P(('dp', 'tensor'))
- grad_norm_gains: float32 [2, 1024], P(None, ('dp', 'tensor'))
- grad_norm_shifts: float32 [4, 1024], P(None, ('dp', 'tensor'))
- grad_w_qkv: float32 [3, 1024, 1024], P(None, 'dp', 'tensor')
- grad_b_qv: float32 [2, 1024], P(None, ('tensor', 'dp'))
- grad_w_out: float32 [1024, 1024], P('tensor', 'dp')
- grad_w_up: float32 [1024, 4096], P('dp', 'tensor')
- grad_up_bias: float32 [4096], P(('tensor', 'dp'))
- grad_w_down: float32 [4096, 1024], P('tensor', 'dp')
All inputs are finite; a program needn't handle non-finite values. No bound on the sum of `image_mask` on one device may be relied on, other than what follows from the above.
Results may differ from a plain program's by a relative error of at most 0.02.
Values may be sent and summed in bfloat16 or wider, within the bound.
No kernel may reach another device: no remote copies, remote signals or barrier semaphores. Data moves between devices by JAX's collectives and lax.ppermute only.
A program may use at most 320 MiB of HBM per device.

v0:
```python
import jax
import jax.numpy as jnp
from jax import lax
from jax.sharding import PartitionSpec as P

HEAD_DIM = 64
VALID = 577
SEQ = 584


def layer_norm(rows_in, gain_row, shift_row):
    center = rows_in - jnp.mean(rows_in, axis=1, keepdims=True)
    inverse = lax.rsqrt(jnp.mean(center * center, axis=1, keepdims=True) + 1e-05)
    scaled = center * inverse
    return (scaled, inverse, scaled * gain_row + shift_row)


def norm_back(grad_norm, scaled, inverse, gain_row):
    grad_hat = grad_norm * gain_row
    first_mean = jnp.mean(grad_hat, axis=1, keepdims=True)
    second_mean = jnp.mean(grad_hat * scaled, axis=1, keepdims=True)
    return inverse * (grad_hat - first_mean - scaled * second_mean)


def per_device(
    tokens,
    cotangent,
    image_mask,
    norm_gains,
    norm_shifts,
    w_qkv,
    b_qv,
    w_out,
    w_up,
    up_bias,
    w_down,
):
    tensor_pos = lax.axis_index("tensor")
    local_rows = tokens.shape[0]
    images_dp = image_mask.shape[0]
    score_scale = HEAD_DIM ** (-0.5)
    qkv_full, out_full, bias_full, gains_full, shifts_full = (
        lax.all_gather(w_qkv, "dp", axis=1, tiled=True),
        lax.all_gather(w_out, "dp", axis=1, tiled=True),
        lax.all_gather(b_qv, "dp", axis=1, tiled=True),
        lax.all_gather(norm_gains, "dp", axis=1, tiled=True),
        lax.all_gather(norm_shifts, "dp", axis=1, tiled=True),
    )
    up_full, down_full, cup_full = (
        lax.all_gather(w_up, "dp", axis=0, tiled=True),
        lax.all_gather(w_down, "dp", axis=1, tiled=True),
        lax.all_gather(up_bias, "dp", axis=0, tiled=True),
    )
    gains = gains_full.astype(jnp.float32)
    shifts = shifts_full.astype(jnp.float32)
    width_here = qkv_full.shape[2]
    heads_here = width_here // HEAD_DIM
    owner_image = (tensor_pos * local_rows + lax.iota(jnp.int32, local_rows)) // SEQ
    row_keep = jnp.sum(
        jnp.where(
            owner_image[:, None] == lax.iota(jnp.int32, images_dp)[None, :], image_mask[None, :], 0
        ),
        axis=1,
    ).astype(jnp.float32)[:, None]
    rows_in = tokens.astype(jnp.float32)
    hat_one, inv_one, normed_one = layer_norm(rows_in, gains[0], shifts[0])
    low_one = normed_one.astype(jnp.bfloat16)
    full_one = lax.all_gather(low_one, "tensor", axis=0, tiled=True)
    work_rows = full_one.shape[0]
    head_shape = (work_rows // SEQ, SEQ, heads_here, HEAD_DIM)
    projected = jnp.einsum("rd,cde->cre", full_one, qkv_full, preferred_element_type=jnp.float32)
    bias_wide = bias_full.astype(jnp.float32)
    queries = (projected[0] + bias_wide[0]).astype(jnp.bfloat16).reshape(head_shape)
    keys_all = projected[1].astype(jnp.bfloat16).reshape(head_shape)
    values = (projected[2] + bias_wide[1]).astype(jnp.bfloat16).reshape(head_shape)
    valid_keys = lax.iota(jnp.int32, SEQ) < VALID

    def scores_of(query_blk, key_blk):
        raw_scores = (
            jnp.einsum("qhd,khd->hqk", query_blk, key_blk, preferred_element_type=jnp.float32)
            * score_scale
        )
        return jnp.where(valid_keys[None, None, :], raw_scores, -1e30)

    def attend(blocks):
        query_blk, key_blk, value_blk = blocks
        scores = scores_of(query_blk, key_blk)
        row_max = jnp.max(scores, axis=2, keepdims=True)
        exponent = jnp.exp(scores - row_max)
        row_total = jnp.sum(exponent, axis=2, keepdims=True)
        attn_probs = (exponent / row_total).astype(jnp.bfloat16)
        result = jnp.einsum(
            "hqk,khd->qhd", attn_probs, value_blk, preferred_element_type=jnp.float32
        )
        return (result.astype(jnp.bfloat16), (row_max + jnp.log(row_total))[:, :, 0])

    attended, log_total = lax.map(attend, (queries, keys_all, values))
    flat_out = attended.reshape(work_rows, width_here)
    attn_part = jnp.dot(flat_out, out_full, preferred_element_type=jnp.float32)
    attn_sum = lax.psum_scatter(
        attn_part.astype(jnp.bfloat16), "tensor", scatter_dimension=0, tiled=True
    ).astype(jnp.float32)
    middle = rows_in + row_keep * (attn_sum + shifts[2])
    hat_two, inv_two, normed_two = layer_norm(middle, gains[1], shifts[1])
    low_two = normed_two.astype(jnp.bfloat16)
    full_two = lax.all_gather(low_two, "tensor", axis=0, tiled=True)
    hidden_pre = jnp.dot(full_two, up_full, preferred_element_type=jnp.float32) + cup_full.astype(
        jnp.float32
    )
    gating = jax.nn.sigmoid(1.702 * hidden_pre)
    activated = (hidden_pre * gating).astype(jnp.bfloat16)
    mlp_part = jnp.dot(activated, down_full, preferred_element_type=jnp.float32)
    mlp_sum = lax.psum_scatter(
        mlp_part.astype(jnp.bfloat16), "tensor", scatter_dimension=0, tiled=True
    ).astype(jnp.float32)
    layer_out = (middle + row_keep * (mlp_sum + shifts[3])).astype(jnp.bfloat16)
    grad_top = cotangent.astype(jnp.float32)
    grad_mlp = row_keep * grad_top
    send_mlp = grad_mlp.astype(jnp.bfloat16)
    mlp_grad_full = lax.all_gather(send_mlp, "tensor", axis=0, tiled=True)
    grad_act = jnp.einsum("rd,fd->rf", mlp_grad_full, down_full, preferred_element_type=jnp.float32)
    grad_pre = grad_act * (gating + 1.702 * hidden_pre * gating * (1.0 - gating))
    low_pre = grad_pre.astype(jnp.bfloat16)
    grad_down = jnp.einsum(
        "rf,rd->fd", activated, mlp_grad_full, preferred_element_type=jnp.float32
    )
    grad_up = jnp.einsum("rd,rf->df", full_two, low_pre, preferred_element_type=jnp.float32)
    grad_cup = jnp.sum(grad_pre, axis=0)
    two_part = jnp.einsum("rf,df->rd", low_pre, up_full, preferred_element_type=jnp.float32)
    grad_two = lax.psum_scatter(
        two_part.astype(jnp.bfloat16), "tensor", scatter_dimension=0, tiled=True
    ).astype(jnp.float32)
    grad_mid = grad_top + norm_back(grad_two, hat_two, inv_two, gains[1])
    grad_attn = row_keep * grad_mid
    send_attn = grad_attn.astype(jnp.bfloat16)
    attn_grad_full = lax.all_gather(send_attn, "tensor", axis=0, tiled=True)
    grad_flat = jnp.einsum(
        "rd,ed->re", attn_grad_full, out_full, preferred_element_type=jnp.float32
    ).astype(jnp.bfloat16)
    grad_wout = jnp.einsum(
        "re,rd->ed", flat_out, attn_grad_full, preferred_element_type=jnp.float32
    )
    grad_heads = grad_flat.reshape(head_shape)

    def attend_back(blocks):
        query_blk, key_blk, value_blk, grad_blk, log_blk = blocks
        attn_probs = jnp.exp(scores_of(query_blk, key_blk) - log_blk[:, :, None])
        grad_probs = jnp.einsum(
            "qhd,khd->hqk", grad_blk, value_blk, preferred_element_type=jnp.float32
        )
        row_dot = jnp.sum(attn_probs * grad_probs, axis=2, keepdims=True)
        grad_scores = (attn_probs * (grad_probs - row_dot)).astype(jnp.bfloat16)
        grad_q = (
            jnp.einsum("hqk,khd->qhd", grad_scores, key_blk, preferred_element_type=jnp.float32)
            * score_scale
        )
        grad_k = (
            jnp.einsum("hqk,qhd->khd", grad_scores, query_blk, preferred_element_type=jnp.float32)
            * score_scale
        )
        grad_v = jnp.einsum(
            "hqk,qhd->khd",
            attn_probs.astype(jnp.bfloat16),
            grad_blk,
            preferred_element_type=jnp.float32,
        )
        return (grad_q, grad_k, grad_v)

    grad_q, grad_k, grad_v = lax.map(
        attend_back, (queries, keys_all, values, grad_heads, log_total)
    )
    grad_proj = jnp.stack([grad_q, grad_k, grad_v]).reshape(3, work_rows, width_here)
    grad_bias_qv = jnp.stack([jnp.sum(grad_proj[0], axis=0), jnp.sum(grad_proj[2], axis=0)])
    low_proj = grad_proj.astype(jnp.bfloat16)
    grad_qkv = jnp.einsum("rd,cre->cde", full_one, low_proj, preferred_element_type=jnp.float32)
    one_part = jnp.einsum("cre,cde->rd", low_proj, qkv_full, preferred_element_type=jnp.float32)
    grad_one = lax.psum_scatter(
        one_part.astype(jnp.bfloat16), "tensor", scatter_dimension=0, tiled=True
    ).astype(jnp.float32)
    grad_in = grad_mid + norm_back(grad_one, hat_one, inv_one, gains[0])
    gain_grads = jnp.stack(
        [jnp.sum(grad_one * hat_one, axis=0), jnp.sum(grad_two * hat_two, axis=0)]
    )
    shift_grads = jnp.stack(
        [
            jnp.sum(grad_one, axis=0),
            jnp.sum(grad_two, axis=0),
            jnp.sum(grad_attn, axis=0),
            jnp.sum(grad_mlp, axis=0),
        ]
    )
    qkv_share, wout_share, bias_share, up_share, down_share, cup_share = (
        lax.psum_scatter(
            grad_qkv.astype(jnp.bfloat16), "dp", scatter_dimension=1, tiled=True
        ).astype(jnp.float32),
        lax.psum_scatter(
            grad_wout.astype(jnp.bfloat16), "dp", scatter_dimension=1, tiled=True
        ).astype(jnp.float32),
        lax.psum_scatter(
            grad_bias_qv.astype(jnp.bfloat16), "dp", scatter_dimension=1, tiled=True
        ).astype(jnp.float32),
        lax.psum_scatter(
            grad_up.astype(jnp.bfloat16), "dp", scatter_dimension=0, tiled=True
        ).astype(jnp.float32),
        lax.psum_scatter(
            grad_down.astype(jnp.bfloat16), "dp", scatter_dimension=1, tiled=True
        ).astype(jnp.float32),
        lax.psum_scatter(
            grad_cup.astype(jnp.bfloat16), "dp", scatter_dimension=0, tiled=True
        ).astype(jnp.float32),
    )
    gain_share, shift_share = (
        lax.psum_scatter(gain_grads, ("dp", "tensor"), scatter_dimension=1, tiled=True),
        lax.psum_scatter(shift_grads, ("dp", "tensor"), scatter_dimension=1, tiled=True),
    )
    return (
        layer_out,
        grad_in.astype(jnp.bfloat16),
        gain_share,
        shift_share,
        qkv_share,
        bias_share,
        wout_share,
        up_share,
        cup_share,
        down_share,
    )


def solution(mesh):
    in_specs = (
        P(("dp", "tensor"), None),
        P(("dp", "tensor"), None),
        P("dp"),
        P(None, "dp"),
        P(None, "dp"),
        P(None, "dp", "tensor"),
        P(None, ("tensor", "dp")),
        P("tensor", "dp"),
        P("dp", "tensor"),
        P(("tensor", "dp")),
        P("tensor", "dp"),
    )
    out_specs = (
        P(("dp", "tensor"), None),
        P(("dp", "tensor"), None),
        P(None, ("dp", "tensor")),
        P(None, ("dp", "tensor")),
        P(None, "dp", "tensor"),
        P(None, ("tensor", "dp")),
        P("tensor", "dp"),
        P("dp", "tensor"),
        P(("tensor", "dp")),
        P("tensor", "dp"),
    )
    return jax.shard_map(
        per_device, mesh=mesh, in_specs=in_specs, out_specs=out_specs, check_vma=False
    )
```

profile of v0, /device:TPU:0, one launch (start us, length us, event | category | flops | bytes accessed | tf_op | source)
XLA Modules:
  0.0 1240.6 jit_solution(2609150840192611639)
XLA Ops:
  8.0 22.4 %all_gather.36 = bf16[2,1024]{1,0:T(2,128)(2,1)S(1)} all-gather(bf16[2,128]{1,0:T(2,128)(2,1)} %param.18), channel_id=1, replica_groups=mesh['dp'=8,'tensor'=4] {'dp'}, dimensions={1}, use_global_device_ids=true | all-gather | bytes 4608 | tf_op jit(solution)/shard_map/all_gather | solution.py:46
  30.3 16.6 %all_gather.37 = bf16[4,1024]{1,0:T(4,128)(2,1)S(1)} all-gather(bf16[4,128]{1,0:T(4,128)(2,1)} %param.19), channel_id=1, replica_groups=mesh['dp'=8,'tensor'=4] {'dp'}, dimensions={1}, use_global_device_ids=true | all-gather | bytes 9216 | tf_op jit(solution)/shard_map/all_gather | solution.py:47
  52.5 18.1 %all-gather = bf16[8,32,2]{1,2,0:T(2,128)(2,1)S(1)} all-gather(bf16[1,32,2]{1,2,0:T(2,128)(2,1)S(1)} %bitcast.216), channel_id=1, replica_groups=mesh['dp'=8,'tensor'=4] {'dp'}, dimensions={0}, use_global_device_ids=true | all-gather | bytes 1152 | tf_op jit(solution)/shard_map/all_gather | solution.py:45
  70.9 27.0 %all_gather.41 = bf16[256,1024]{1,0:T(8,128)(2,1)S(1)} all-gather(bf16[256,128]{1,0:T(8,128)(2,1)S(1)} %copy-done.18), channel_id=1, replica_groups=mesh['dp'=8,'tensor'=4] {'dp'}, dimensions={1}, use_global_device_ids=true | all-gather | bytes 589824 | tf_op jit(solution)/shard_map/all_gather | solution.py:44
  97.9 6.2 convolution_bitcast_fusion
  137.5 29.4 %while.28 = (s32[]{:T(128)}, bf16[4,584,4,64]{1,3,2,0:T(8,128)(2,1)}, f32[4,4,584]{2,1,0:T(4,128)S(1)}, bf16[4,584,4,64]{1,3,2,0:T(8,128)(2,1)}, bf16[4,584,4,64...) while((s32[]{:T(128)}, bf16[4,584,4,64]{1,3,2,0:T(8,128)(2,1)}, ...), condition=%wide.region_6.7_spmd.clone, body=%wide.region_3.6_spmd.clone.sunk | while | flops 365759776 | bytes 17763760 | solution.py:97
  180.0 45.5 %reduce-scatter.24.cloned.1.call-done = bf16[584,1024]{1,0:T(8,128)(2,1)} async-done(((bf16[2336,1024]{1,0:T(8,128)(2,1)}), bf16[584,1024]{1,0:T(8,128)(2,1)}) %reduce-scatter.24.cloned.1.call-update) | async-done | bytes 1196048 | tf_op jit(solution)/shard_map/reduce_scatter | solution.py:100
  233.9 20.4 %all-gather.1 = bf16[8,1,128]{2,1,0:T(2,128)(2,1)S(1)} all-gather(bf16[1,1,128]{2,1,0:T(2,128)(2,1)S(1)} %bitcast.217), channel_id=1, replica_groups=mesh['dp'=8,'tensor'=4] {'dp'}, dimensions={0}, use_global_device_ids=true | all-gather | bytes 2304 | tf_op jit(solution)/shard_map/all_gather | solution.py:52
  254.3 22.8 %all-gather.16.cloned.1.call-done = bf16[1024,1024]{1,0:T(8,128)(2,1)} async-done(((bf16[128,1024]{1,0:T(8,128)(2,1)}), bf16[1024,1024]{1,0:T(8,128)(2,1)}) %all-gather.16.cloned.1.call-update) | async-done | bytes 2097168 | tf_op jit(solution)/shard_map/all_gather | solution.py:50
  277.1 38.4 %all-gather.14.cloned.1.call-done = bf16[2336,1024]{1,0:T(8,128)(2,1)} async-done(((bf16[584,1024]{1,0:T(8,128)(2,1)}), bf16[2336,1024]{1,0:T(8,128)(2,1)}) %all-gather.14.cloned.1.call-update) | async-done | bytes 4784144 | tf_op jit(solution)/shard_map/all_gather | solution.py:106
  315.5 12.6 %multiply_convert_fusion.1 = (bf16[2336,1024]{1,0:T(8,128)(2,1)}, f32[2336,1024]{1,0:T(8,128)}) fusion(f32[1024]{0:T(1024)S(1)} %bitcast.214, bf16[2336,1024]{1,0:T(8,128)(2,1)} %all-gather.14.cloned.1.call-done, bf16[1024,1024]{1,0:T(8,128)(2,1)} %all-gather.16.cloned.1.call-done), kind=kOutput, calls=%fused_computation.65 | convolution fusion | flops 4915691520 | bytes 21237760 | tf_op jit(solution)/shard_map/dot_general | solution.py:107
  328.1 40.6 %all-gather.18.cloned.1.call-done = bf16[1024,1024]{1,0:T(8,128)(2,1)} async-done(((bf16[1024,128]{1,0:T(8,128)(2,1)}), bf16[1024,1024]{1,0:T(8,128)(2,1)}) %all-gather.18.cloned.1.call-update) | async-done | bytes 2097168 | tf_op jit(solution)/shard_map/all_gather | solution.py:51
  368.8 38.3 %all-gather.20.cloned.1.call-done = bf16[2336,1024]{1,0:T(8,128)(2,1)} async-done(((bf16[584,1024]{1,0:T(8,128)(2,1)}), bf16[2336,1024]{1,0:T(8,128)(2,1)}) %all-gather.20.cloned.1.call-update) | async-done | bytes 4784144 | tf_op jit(solution)/shard_map/all_gather | solution.py:120
  407.0 12.7 %fusion.105 = (bf16[1024]{0:T(1024)(128)(2,1)S(1)}, bf16[2336,1024]{1,0:T(8,128)(2,1)S(1)}) fusion(f32[2336,1024]{1,0:T(8,128)} %get-tuple-element.329, f32[1024]{0:T(1024)S(1)} %bitcast.215, bf16[2336,1024]{1,0:T(8,128)(2,1)} %all-gather.20.cloned.1.call-done, bf16[1024,1024]{1,0:T(8,128)(2,1)} %all-gather.18.cloned.1.call-done), kind=kOutput, calls=%fused_computation.159 | convolution fusion | flops 4927650816 | bytes 21239808 | tf_op jit(solution)/shard_map/rd,fd->rf/dot_general | solution.py:121
  421.9 6.9 convolution_convert_fusion
  428.9 9.6 convolution_convert_fusion.1
  438.7 38.5 %reduce-scatter.28.cloned.1.call-done = bf16[584,1024]{1,0:T(8,128)(2,1)} async-done(((bf16[2336,1024]{1,0:T(8,128)(2,1)}), bf16[584,1024]{1,0:T(8,128)(2,1)}) %reduce-scatter.28.cloned.1.call-update) | async-done | bytes 1196048 | tf_op jit(solution)/shard_map/reduce_scatter | solution.py:130
  480.7 47.3 %reduce-scatter.26.cloned.1.call-done = bf16[584,1024]{1,0:T(8,128)(2,1)} async-done(((bf16[2336,1024]{1,0:T(8,128)(2,1)}), bf16[584,1024]{1,0:T(8,128)(2,1)}) %reduce-scatter.26.cloned.1.call-update) | async-done | bytes 1196048 | tf_op jit(solution)/shard_map/reduce_scatter | solution.py:113
  535.1 10.0 convolution_convert_fusion.4
  549.1 10.0 fusion.89
  559.4 13.6 %all-gather.22.cloned.1.call-done = bf16[2336,1024]{1,0:T(8,128)(2,1)} async-done(((bf16[584,1024]{1,0:T(8,128)(2,1)}), bf16[2336,1024]{1,0:T(8,128)(2,1)}) %all-gather.22.cloned.1.call-update) | async-done | bytes 4784144 | tf_op jit(solution)/shard_map/all_gather | solution.py:136
  583.3 53.3 %while.29 = (s32[]{:T(128)}, f32[4,584,4,64]{1,3,2,0:T(8,128)}, bf16[4,584,4,64]{1,3,2,0:T(8,128)(2,1)}, f32[4,584,4,64]{1,3,2,0:T(8,128)}, bf16[4,584,4,64]{1,3...) while((s32[]{:T(128)}, f32[4,584,4,64]{1,3,2,0:T(8,128)}, ...), condition=%wide.region_16.17_spmd.clone, body=%wide.region_14.16_spmd.clone.sunk | while | flops 893863936 | bytes 60922836 | solution.py:169
  636.6 5.8 fusion.101
  676.0 9.0 fusion.95
  689.6 8.6 bitcast_convert_fusion
  700.1 21.7 %all-reduce = bf16[1024]{0:T(1024)(128)(2,1)S(1)} all-reduce(bf16[1024]{0:T(1024)(128)(2,1)S(1)} %get-tuple-element.330), channel_id=12, replica_groups=mesh['dp'=8,'tensor'=4] {'dp'}, use_global_device_ids=true, to_apply=%region_35.36.clone | all-reduce | flops 1024 | bytes 4096
  726.1 54.3 %reduce-scatter.40.cloned.1.call-done = bf16[32,2]{1,0:T(8,128)(2,1)} async-done(((bf16[256,2]{1,0:T(8,128)(2,1)}), bf16[32,2]{1,0:T(8,128)(2,1)}) %reduce-scatter.40.cloned.1.call-update) | async-done | bytes 144
  781.7 63.2 %reduce-scatter.42.cloned.1.call-done = bf16[128,256]{1,0:T(8,128)(2,1)} async-done(((bf16[1024,256]{1,0:T(8,128)(2,1)}), bf16[128,256]{1,0:T(8,128)(2,1)}) %reduce-scatter.42.cloned.1.call-update) | async-done | bytes 65552
  846.5 65.7 %reduce-scatter.38.cloned.1.call-done = bf16[128,768]{1,0:T(8,128)(2,1)} async-done(((bf16[1024,768]{1,0:T(8,128)(2,1)}), bf16[128,768]{1,0:T(8,128)(2,1)}) %reduce-scatter.38.cloned.1.call-update) | async-done | bytes 196624
  914.3 47.6 %reduce-scatter.30.cloned.1.call-done = bf16[584,1024]{1,0:T(8,128)(2,1)} async-done(((bf16[2336,1024]{1,0:T(8,128)(2,1)}), bf16[584,1024]{1,0:T(8,128)(2,1)}) %reduce-scatter.30.cloned.1.call-update) | async-done | bytes 1196048 | tf_op jit(solution)/shard_map/reduce_scatter | solution.py:177
  970.3 129.4 %reduce-scatter.34.cloned.1.call-done = f32[32,2]{1,0:T(8,128)} async-done(((f32[1024,2]{1,0:T(8,128)}), f32[32,2]{1,0:T(8,128)}) %reduce-scatter.34.cloned.1.call-update) | async-done | bytes 272
  1101.1 130.8 %reduce-scatter.36.cloned.1.call-done = f32[32,4]{1,0:T(8,128)} async-done(((f32[1024,4]{1,0:T(8,128)}), f32[32,4]{1,0:T(8,128)}) %reduce-scatter.36.cloned.1.call-update) | async-done | bytes 528
  (251 shorter events, 230.4 us)
Async XLA Ops:
  7.2 43.7 %copy-start = (bf16[584,1024]{1,0:T(8,128)(2,1)S(1)}, bf16[584,1024]{1,0:T(8,128)(2,1)}, u32[]{:S(2)}) copy-start(bf16[584,1024]{1,0:T(8,128)(2,1)} %param.15) | copy-start | bytes 3588100
  7.2 90.8 %all-gather.12.cloned.1.call-start = ((), (), s32[]{:S(2)}) async-start(), calls=%async_computation.12 | async-start | bytes 1769472 | tf_op jit(solution)/shard_map/all_gather | solution.py:43
  7.9 90.0 %all-gather.10.cloned.1.call-start = ((), (), s32[]{:S(2)}) async-start(), calls=%async_computation.11 | async-start | bytes 5980160 | tf_op jit(solution)/shard_map/all_gather | solution.py:68
  48.5 4.1 copy-start.20
  48.5 22.4 %copy-start.18 = (bf16[256,128]{1,0:T(8,128)(2,1)S(1)}, bf16[256,128]{1,0:T(8,128)(2,1)}, u32[]{:S(2)}) copy-start(bf16[256,128]{1,0:T(8,128)(2,1)} %param.22) | copy-start | bytes 196612
  52.5 173.1 %reduce-scatter.24.cloned.1.call-start = ((), (), s32[]{:S(2)}) async-start(), calls=%async_computation.13 | async-start | bytes 5980160 | tf_op jit(solution)/shard_map/reduce_scatter | solution.py:100
  167.0 7.4 copy-start.2
  179.3 97.9 %all-gather.16.cloned.1.call-start = ((), (), s32[]{:S(2)}) async-start(), calls=%async_computation.15 | async-start | bytes 2359296 | tf_op jit(solution)/shard_map/all_gather | solution.py:50
  179.8 135.7 %all-gather.14.cloned.1.call-start = ((), (), s32[]{:S(2)}) async-start(), calls=%async_computation.14 | async-start | bytes 5980160 | tf_op jit(solution)/shard_map/all_gather | solution.py:106
  230.7 3.2 copy-start.22
  232.5 136.3 %all-gather.18.cloned.1.call-start = ((), (), s32[]{:S(2)}) async-start(), calls=%async_computation.16 | async-start | bytes 2359296 | tf_op jit(solution)/shard_map/all_gather | solution.py:51
  233.1 173.9 %all-gather.20.cloned.1.call-start = ((), (), s32[]{:S(2)}) async-start(), calls=%async_computation.18 | async-start | bytes 5980160 | tf_op jit(solution)/shard_map/all_gather | solution.py:120
  233.8 243.4 %reduce-scatter.28.cloned.1.call-start = ((), (), s32[]{:S(2)}) async-start(), calls=%async_computation.19 | async-start | bytes 5980160 | tf_op jit(solution)/shard_map/reduce_scatter | solution.py:130
  407.0 14.9 %copy-start.23 = (bf16[1024,1024]{1,0:T(8,128)(2,1)S(1)}, bf16[1024,1024]{1,0:T(8,128)(2,1)}, u32[]{:S(2)}) copy-start(bf16[1024,1024]{1,0:T(8,128)(2,1)} %all-gather.16.cloned.1.call-done) | copy-start | bytes 6291460
  428.8 99.3 %reduce-scatter.26.cloned.1.call-start = ((), (), s32[]{:S(2)}) async-start(), calls=%async_computation.17 | async-start | bytes 5980160 | tf_op jit(solution)/shard_map/reduce_scatter | solution.py:113
  438.4 89.6 %copy-start.19 = (f32[1,1024]{1,0:T(1,128)S(1)}, f32[1,1024]{1,0:T(1,128)}, u32[]{:S(2)}) copy-start(f32[1,1024]{1,0:T(1,128)} %get-tuple-element.320) | copy-start | bytes 12292
  438.5 134.6 %all-gather.22.cloned.1.call-start = ((), (), s32[]{:S(2)}) async-start(), calls=%async_computation.20 | async-start | bytes 5980160 | tf_op jit(solution)/shard_map/all_gather | solution.py:136
  535.0 187.3 %reduce-scatter.44.cloned.1.call-start = ((), (), s32[]{:S(2)}) async-start(), calls=%async_computation.28 | async-start | bytes 2359296
  549.1 175.2 %reduce-scatter.32.cloned.1.call-start = ((), (), s32[]{:S(2)}) async-start(), calls=%async_computation.22 | async-start | bytes 2359296 | tf_op jit(solution)/shard_map/reduce_scatter | solution.py:202
  559.2 221.2 %reduce-scatter.40.cloned.1.call-start = ((), (), s32[]{:S(2)}) async-start(), calls=%async_computation.26 | async-start | bytes 73728
  578.9 4.3 copy-start.3
  646.0 5.0 copy-start.5
  650.7 194.2 %reduce-scatter.42.cloned.1.call-start = ((), (), s32[]{:S(2)}) async-start(), calls=%async_computation.27 | async-start | bytes 589824
  651.0 4.0 copy-start.9
  672.5 239.8 %reduce-scatter.38.cloned.1.call-start = ((), (), s32[]{:S(2)}) async-start(), calls=%async_computation.25 | async-start | bytes 1769472
  689.6 272.4 %reduce-scatter.30.cloned.1.call-start = ((), (), s32[]{:S(2)}) async-start(), calls=%async_computation.21 | async-start | bytes 5980160 | tf_op jit(solution)/shard_map/reduce_scatter | solution.py:177
  698.2 263.8 %copy-start.13 = (f32[584]{0:T(1024)S(1)}, f32[584]{0:T(1024)}, u32[]{:S(2)}) copy-start(f32[584]{0:T(1024)} %copy-done.12) | copy-start | bytes 7012
  698.2 263.8 %copy-start.15 = (f32[584]{0:T(1024)S(1)}, f32[584]{0:T(1024)}, u32[]{:S(2)}) copy-start(f32[584]{0:T(1024)} %copy-done.14) | copy-start | bytes 7012
  698.2 263.7 %copy-start.17 = (f32[1,1024]{1,0:T(1,128)S(1)}, f32[1,1024]{1,0:T(1,128)}, u32[]{:S(2)}) copy-start(f32[1,1024]{1,0:T(1,128)} %copy-done.16) | copy-start | bytes 12292
  698.2 401.5 %reduce-scatter.34.cloned.1.call-start = ((), (), s32[]{:S(2)}) async-start(), calls=%async_computation.23 | async-start | bytes 540672
  962.0 4.8 copy-start.8
  965.6 266.3 %reduce-scatter.36.cloned.1.call-start = ((), (), s32[]{:S(2)}) async-start(), calls=%async_computation.24 | async-start | bytes 540672
  (21 other events, 40.5 us)
Sparse Core Ops, SparseCore 0:
  10.2 46.6 all-gather.11
  59.1 36.6 all-gather.9
  179.4 46.1 reduce-scatter.23
  227.7 49.3 all-gather.15
  279.2 36.3 all-gather.13
  317.6 51.0 all-gather.17
  371.0 35.9 all-gather.19
  428.9 48.2 reduce-scatter.27
  479.8 48.2 reduce-scatter.25
  535.1 37.8 all-gather.21
  577.0 67.9 reduce-scatter.43
  648.8 66.9 reduce-scatter.31
  720.2 60.1 reduce-scatter.39
  784.0 60.8 reduce-scatter.41
  848.2 64.0 reduce-scatter.37
  914.8 47.1 reduce-scatter.29
  965.7 133.9 reduce-scatter.33
  1101.9 129.9 reduce-scatter.35
where the time goes:
time: 1250 us; the launch traced here: 1240 us
  waiting for transfers between devices  779 us (62%)
  matrix products  167 us (13%)
  blocking collectives  126 us (10%)
  local copies, waits for them, and re-layouts  95.9 us (8%)
  other arithmetic  55 us (4%)
  between operations  15.9 us (1%)
    unnamed x24, waiting for transfers between devices  446 us
    reduce_scatter x1, waiting for transfers between devices, per_device(): lax.psum_scatter(one_part.astype(jnp.bfloat16), 'tensor', scatter_dimensi...  47.6 us
    reduce_scatter x1, waiting for transfers between devices, per_device(): lax.psum_scatter(mlp_part.astype(jnp.bfloat16), 'tensor', scatter_dimensi...  47.3 us
    reduce_scatter x1, waiting for transfers between devices, per_device(): lax.psum_scatter(attn_part.astype(jnp.bfloat16), 'tensor', scatter_dimens...  45.5 us
    all_gather x1, waiting for transfers between devices, per_device(): lax.all_gather(w_down, 'dp', axis=1, tiled=True)  40.6 us
    reduce_scatter x1, waiting for transfers between devices, per_device(): lax.psum_scatter(two_part.astype(jnp.bfloat16), 'tensor', scatter_dimensi...  38.5 us
    unnamed x68, local copies, waits for them, and re-layouts  38.5 us
    all_gather x1, waiting for transfers between devices, per_device(): full_two = lax.all_gather(low_two, 'tensor', axis=0, tiled=True)  38.4 us
  transfers between devices with their start and end apart: 18, of which 14 were waited for; matrix products, arithmetic and copies ran while one was open for 16% of the time, Pallas kernels for 0%

commit v1 on v0

--- a/solution.py
+++ b/solution.py
@@ -6,6 +6,17 @@
 HEAD_DIM = 64
 VALID = 577
 SEQ = 584
+
+
+def collect(x, axis, dim):
+    ways = lax.axis_size(axis)
+    pieces = [x]
+    for far in range(1, ways):
+        pieces.append(
+            lax.ppermute(pieces[far - 1], axis, [(d, (d - 1) % ways) for d in range(ways)])
+        )
+    line = jnp.concatenate(pieces, axis=dim)
+    return jnp.roll(line, lax.axis_index(axis) * x.shape[dim], axis=dim)
 
 
 def layer_norm(rows_in, gain_row, shift_row):
@@ -103,7 +114,7 @@
     middle = rows_in + row_keep * (attn_sum + shifts[2])
     hat_two, inv_two, normed_two = layer_norm(middle, gains[1], shifts[1])
     low_two = normed_two.astype(jnp.bfloat16)
-    full_two = lax.all_gather(low_two, "tensor", axis=0, tiled=True)
+    full_two = collect(low_two, "tensor", 0)
     hidden_pre = jnp.dot(full_two, up_full, preferred_element_type=jnp.float32) + cup_full.astype(
         jnp.float32
     )

time: 1250 us -> 1210 us (0.968)
  waiting for transfers between devices: 779 us -> 715 us
  local copies, waits for them, and re-layouts: 95.9 us -> 115 us
    all_gather x1 -> x0, waiting for transfers between devices: 38.4 us -> none  [per_device(): full_two = lax.all_gather(low_two, 'tensor', axis=0, tiled=True)]
    ppermute x0 -> x3, waiting for transfers between devices: none -> 27.8 us  [collect(): lax.ppermute(pieces[far - 1], axis, [(d, (d - 1) % ways) for d in range(w...]
    all_gather x1, waiting for transfers between devices: 40.6 us -> 14.4 us  [per_device(): lax.all_gather(w_down, 'dp', axis=1, tiled=True)]
    all_gather x1, waiting for transfers between devices: 22.8 us -> 0.01 us  [per_device(): lax.all_gather(w_up, 'dp', axis=0, tiled=True)]
    unnamed x68 -> x84, local copies, waits for them, and re-layouts: 38.5 us -> 52.1 us
    unnamed x24 -> x23, waiting for transfers between devices: 446 us -> 442 us
  transfers between devices with their start and end apart: 18 -> 20, of which waited for: 14 -> 14; matrix products, arithmetic and copies ran while one was open for 16% -> 18% of each run, Pallas kernels for 0% -> 0%
where the time goes in v1:
time: 1210 us; the launch traced here: 1200 us
  waiting for transfers between devices  715 us (59%)
  matrix products  167 us (14%)
  blocking collectives  126 us (10%)
  local copies, waits for them, and re-layouts  115 us (10%)
  other arithmetic  55.4 us (5%)
  between operations  15.5 us (1%)
    unnamed x23, waiting for transfers between devices  442 us
    unnamed x84, local copies, waits for them, and re-layouts  52.1 us
    reduce_scatter x1, waiting for transfers between devices, per_device(): lax.psum_scatter(one_part.astype(jnp.bfloat16), 'tensor', scatter_dimensi...  47.6 us
    reduce_scatter x1, waiting for transfers between devices, per_device(): lax.psum_scatter(mlp_part.astype(jnp.bfloat16), 'tensor', scatter_dimensi...  47.3 us
    reduce_scatter x1, waiting for transfers between devices, per_device(): lax.psum_scatter(attn_part.astype(jnp.bfloat16), 'tensor', scatter_dimens...  44.9 us
    reduce_scatter x1, waiting for transfers between devices, per_device(): lax.psum_scatter(two_part.astype(jnp.bfloat16), 'tensor', scatter_dimensi...  38.6 us
    all_gather x1, waiting for transfers between devices, per_device(): mlp_grad_full = lax.all_gather(send_mlp, 'tensor', axis=0, tiled=True)  38.1 us
    ppermute x3, waiting for transfers between devices, collect(): lax.ppermute(pieces[far - 1], axis, [(d, (d - 1) % ways) for d in range(w...  27.8 us
  transfers between devices with their start and end apart: 20, of which 14 were waited for; matrix products, arithmetic and copies ran while one was open for 18% of the time, Pallas kernels for 0%

profile of v1, /device:TPU:0, one launch (start us, length us, event | category | flops | bytes accessed | tf_op | source)
XLA Modules:
  0.0 1199.9 jit_solution(10703574277996962256)
XLA Ops:
  8.0 22.4 %all_gather.33 = bf16[2,1024]{1,0:T(2,128)(2,1)S(1)} all-gather(bf16[2,128]{1,0:T(2,128)(2,1)} %param.18), channel_id=1, replica_groups=mesh['dp'=8,'tensor'=4] {'dp'}, dimensions={1}, use_global_device_ids=true | all-gather | bytes 4608 | tf_op jit(solution)/shard_map/all_gather | solution.py:57
  30.3 16.6 %all_gather.34 = bf16[4,1024]{1,0:T(4,128)(2,1)S(1)} all-gather(bf16[4,128]{1,0:T(4,128)(2,1)} %param.19), channel_id=1, replica_groups=mesh['dp'=8,'tensor'=4] {'dp'}, dimensions={1}, use_global_device_ids=true | all-gather | bytes 9216 | tf_op jit(solution)/shard_map/all_gather | solution.py:58
  52.5 18.1 %all-gather = bf16[8,32,2]{1,2,0:T(2,128)(2,1)S(1)} all-gather(bf16[1,32,2]{1,2,0:T(2,128)(2,1)S(1)} %bitcast.214), channel_id=1, replica_groups=mesh['dp'=8,'tensor'=4] {'dp'}, dimensions={0}, use_global_device_ids=true | all-gather | bytes 1152 | tf_op jit(solution)/shard_map/all_gather | solution.py:56
  70.9 27.0 %all_gather.38 = bf16[256,1024]{1,0:T(8,128)(2,1)S(1)} all-gather(bf16[256,128]{1,0:T(8,128)(2,1)S(1)} %copy-done.23), channel_id=1, replica_groups=mesh['dp'=8,'tensor'=4] {'dp'}, dimensions={1}, use_global_device_ids=true | all-gather | bytes 589824 | tf_op jit(solution)/shard_map/all_gather | solution.py:55
  97.9 6.2 convolution_bitcast_fusion
  137.6 29.2 %while.28 = (s32[]{:T(128)}, bf16[4,584,4,64]{1,3,2,0:T(8,128)(2,1)}, f32[4,4,584]{2,1,0:T(4,128)S(1)}, bf16[4,584,4,64]{1,3,2,0:T(8,128)(2,1)}, bf16[4,584,4,64...) while((s32[]{:T(128)}, bf16[4,584,4,64]{1,3,2,0:T(8,128)(2,1)}, ...), condition=%wide.region_6.7_spmd.clone, body=%wide.region_3.6_spmd.clone.sunk | while | flops 365759776 | bytes 17763752 | solution.py:108
  180.5 44.9 %reduce-scatter.24.cloned.1.call-done = bf16[584,1024]{1,0:T(8,128)(2,1)} async-done(((bf16[2336,1024]{1,0:T(8,128)(2,1)}), bf16[584,1024]{1,0:T(8,128)(2,1)}) %reduce-scatter.24.cloned.1.call-update) | async-done | bytes 1196048 | tf_op jit(solution)/shard_map/reduce_scatter | solution.py:111
  232.5 13.9 %collective-permute-done = bf16[584,1024]{1,0:T(8,128)(2,1)S(1)} collective-permute-done((bf16[584,1024]{1,0:T(8,128)(2,1)S(1)}, bf16[584,1024]{1,0:T(8,128)(2,1)S(1)}, u32[]{:S(2)}, u32[]{:S(2)}) %collective-permute-start) | collective-permute-done | bytes 1196064 | tf_op jit(solution)/shard_map/ppermute | solution.py:16
  249.7 13.9 %collective-permute-done.1 = bf16[584,1024]{1,0:T(8,128)(2,1)} collective-permute-done((bf16[584,1024]{1,0:T(8,128)(2,1)S(1)}, bf16[584,1024]{1,0:T(8,128)(2,1)}, u32[]{:S(2)}, u32[]{:S(2)}) %collective-permute-start.1) | collective-permute-done | bytes 1196064 | tf_op jit(solution)/shard_map/ppermute | solution.py:16
  265.9 20.4 %all-gather.1 = bf16[8,1,128]{2,1,0:T(2,128)(2,1)S(1)} all-gather(bf16[1,1,128]{2,1,0:T(2,128)(2,1)S(1)} %bitcast.215), channel_id=1, replica_groups=mesh['dp'=8,'tensor'=4] {'dp'}, dimensions={0}, use_global_device_ids=true | all-gather | bytes 2304 | tf_op jit(solution)/shard_map/all_gather | solution.py:63
  300.8 13.4 %multiply_convert_fusion.1 = (bf16[2336,1024]{1,0:T(8,128)(2,1)}, f32[2336,1024]{1,0:T(8,128)}) fusion(f32[1024]{0:T(1024)S(1)} %bitcast.212, bf16[1024,1024]{1,0:T(8,128)(2,1)} %all-gather.13.cloned.1.call-done, bf16[4672,1024]{1,0:T(8,128)(2,1)} %constant_dynamic-update-slice_fusion, s32[]{:T(128)S(6)} %select_n.36), kind=kOutput, calls=%fused_computation.65 | convolution fusion | flops 4915691520 | bytes 21237764 | tf_op jit(solution)/shard_map/dot_general | solution.py:118
  314.2 14.4 %all-gather.15.cloned.1.call-done = bf16[1024,1024]{1,0:T(8,128)(2,1)} async-done(((bf16[1024,128]{1,0:T(8,128)(2,1)}), bf16[1024,1024]{1,0:T(8,128)(2,1)}) %all-gather.15.cloned.1.call-update) | async-done | bytes 2097168 | tf_op jit(solution)/shard_map/all_gather | solution.py:62
  328.6 38.1 %all-gather.17.cloned.1.call-done = bf16[2336,1024]{1,0:T(8,128)(2,1)} async-done(((bf16[584,1024]{1,0:T(8,128)(2,1)}), bf16[2336,1024]{1,0:T(8,128)(2,1)}) %all-gather.17.cloned.1.call-update) | async-done | bytes 4784144 | tf_op jit(solution)/shard_map/all_gather | solution.py:131
  366.8 12.7 %fusion.112 = (bf16[1024]{0:T(1024)(128)(2,1)S(1)}, bf16[2336,1024]{1,0:T(8,128)(2,1)S(1)}) fusion(f32[2336,1024]{1,0:T(8,128)} %get-tuple-element.331, f32[1024]{0:T(1024)S(1)} %bitcast.213, bf16[2336,1024]{1,0:T(8,128)(2,1)} %all-gather.17.cloned.1.call-done, bf16[1024,1024]{1,0:T(8,128)(2,1)} %all-gather.15.cloned.1.call-done), kind=kOutput, calls=%fused_computation.172 | convolution fusion | flops 4927650816 | bytes 21239808 | tf_op jit(solution)/shard_map/rd,fd->rf/dot_general | solution.py:132
  381.6 6.8 convolution_convert_fusion
  388.5 9.7 convolution_convert_fusion.1
  398.3 38.6 %reduce-scatter.28.cloned.1.call-done = bf16[584,1024]{1,0:T(8,128)(2,1)} async-done(((bf16[2336,1024]{1,0:T(8,128)(2,1)}), bf16[584,1024]{1,0:T(8,128)(2,1)}) %reduce-scatter.28.cloned.1.call-update) | async-done | bytes 1196048 | tf_op jit(solution)/shard_map/reduce_scatter | solution.py:141
  440.4 47.3 %reduce-scatter.26.cloned.1.call-done = bf16[584,1024]{1,0:T(8,128)(2,1)} async-done(((bf16[2336,1024]{1,0:T(8,128)(2,1)}), bf16[584,1024]{1,0:T(8,128)(2,1)}) %reduce-scatter.26.cloned.1.call-update) | async-done | bytes 1196048 | tf_op jit(solution)/shard_map/reduce_scatter | solution.py:124
  494.6 10.0 convolution_convert_fusion.4
  508.7 9.9 fusion.92
  518.7 13.9 %all-gather.19.cloned.1.call-done = bf16[2336,1024]{1,0:T(8,128)(2,1)} async-done(((bf16[584,1024]{1,0:T(8,128)(2,1)}), bf16[2336,1024]{1,0:T(8,128)(2,1)}) %all-gather.19.cloned.1.call-update) | async-done | bytes 4784144 | tf_op jit(solution)/shard_map/all_gather | solution.py:147
  543.0 57.9 %while.29 = (s32[]{:T(128)}, f32[4,584,4,64]{1,3,2,0:T(8,128)}, bf16[4,584,4,64]{1,3,2,0:T(8,128)(2,1)}, f32[4,584,4,64]{1,3,2,0:T(8,128)}, bf16[4,584,4,64]{1,3...) while((s32[]{:T(128)}, f32[4,584,4,64]{1,3,2,0:T(8,128)}, ...), condition=%wide.region_16.17_spmd.clone, body=%wide.region_14.16_spmd.clone.sunk | while | flops 893863936 | bytes 60922828 | solution.py:180
  600.8 5.8 fusion.108
  639.4 8.9 fusion.100
  652.9 8.6 bitcast_convert_fusion
  663.4 21.4 %all-reduce = bf16[1024]{0:T(1024)(128)(2,1)S(1)} all-reduce(bf16[1024]{0:T(1024)(128)(2,1)S(1)} %get-tuple-element.332), channel_id=12, replica_groups=mesh['dp'=8,'tensor'=4] {'dp'}, use_global_device_ids=true, to_apply=%region_35.36.clone | all-reduce | flops 1024 | bytes 4096
  689.1 50.5 %reduce-scatter.40.cloned.1.call-done = bf16[32,2]{1,0:T(8,128)(2,1)} async-done(((bf16[256,2]{1,0:T(8,128)(2,1)}), bf16[32,2]{1,0:T(8,128)(2,1)}) %reduce-scatter.40.cloned.1.call-update) | async-done | bytes 144
  741.0 63.9 %reduce-scatter.42.cloned.1.call-done = bf16[128,256]{1,0:T(8,128)(2,1)} async-done(((bf16[1024,256]{1,0:T(8,128)(2,1)}), bf16[128,256]{1,0:T(8,128)(2,1)}) %reduce-scatter.42.cloned.1.call-update) | async-done | bytes 65552
  806.6 65.6 %reduce-scatter.38.cloned.1.call-done = bf16[128,768]{1,0:T(8,128)(2,1)} async-done(((bf16[1024,768]{1,0:T(8,128)(2,1)}), bf16[128,768]{1,0:T(8,128)(2,1)}) %reduce-scatter.38.cloned.1.call-update) | async-done | bytes 196624
  874.3 47.6 %reduce-scatter.30.cloned.1.call-done = bf16[584,1024]{1,0:T(8,128)(2,1)} async-done(((bf16[2336,1024]{1,0:T(8,128)(2,1)}), bf16[584,1024]{1,0:T(8,128)(2,1)}) %reduce-scatter.30.cloned.1.call-update) | async-done | bytes 1196048 | tf_op jit(solution)/shard_map/reduce_scatter | solution.py:188
  930.2 129.5 %reduce-scatter.34.cloned.1.call-done = f32[32,2]{1,0:T(8,128)} async-done(((f32[1024,2]{1,0:T(8,128)}), f32[32,2]{1,0:T(8,128)}) %reduce-scatter.34.cloned.1.call-update) | async-done | bytes 272
  1061.0 130.5 %reduce-scatter.36.cloned.1.call-done = f32[32,4]{1,0:T(8,128)} async-done(((f32[1024,4]{1,0:T(8,128)}), f32[32,4]{1,0:T(8,128)}) %reduce-scatter.36.cloned.1.call-update) | async-done | bytes 528
  (271 shorter events, 253.3 us)
Async XLA Ops:
  7.2 43.7 %copy-start = (bf16[584,1024]{1,0:T(8,128)(2,1)S(1)}, bf16[584,1024]{1,0:T(8,128)(2,1)}, u32[]{:S(2)}) copy-start(bf16[584,1024]{1,0:T(8,128)(2,1)} %param.15) | copy-start | bytes 3588100
  7.2 90.8 %all-gather.11.cloned.1.call-start = ((), (), s32[]{:S(2)}) async-start(), calls=%async_computation.12 | async-start | bytes 1769472 | tf_op jit(solution)/shard_map/all_gather | solution.py:54
  7.9 90.0 %all-gather.9.cloned.1.call-start = ((), (), s32[]{:S(2)}) async-start(), calls=%async_computation.11 | async-start | bytes 5980160 | tf_op jit(solution)/shard_map/all_gather | solution.py:79
  48.5 22.4 %copy-start.23 = (bf16[256,128]{1,0:T(8,128)(2,1)S(1)}, bf16[256,128]{1,0:T(8,128)(2,1)}, u32[]{:S(2)}) copy-start(bf16[256,128]{1,0:T(8,128)(2,1)} %param.22) | copy-start | bytes 196612
  52.5 173.0 %reduce-scatter.24.cloned.1.call-start = ((), (), s32[]{:S(2)}) async-start(), calls=%async_computation.13 | async-start | bytes 5980160 | tf_op jit(solution)/shard_map/reduce_scatter | solution.py:111
  166.8 7.4 copy-start.2
  179.1 121.7 %all-gather.13.cloned.1.call-start = ((), (), s32[]{:S(2)}) async-start(), calls=%async_computation.14 | async-start | bytes 2359296 | tf_op jit(solution)/shard_map/all_gather | solution.py:61
  179.7 148.9 %all-gather.15.cloned.1.call-start = ((), (), s32[]{:S(2)}) async-start(), calls=%async_computation.15 | async-start | bytes 2359296 | tf_op jit(solution)/shard_map/all_gather | solution.py:62
  180.3 186.4 %all-gather.17.cloned.1.call-start = ((), (), s32[]{:S(2)}) async-start(), calls=%async_computation.17 | async-start | bytes 5980160 | tf_op jit(solution)/shard_map/all_gather | solution.py:131
  230.6 206.3 %reduce-scatter.28.cloned.1.call-start = ((), (), s32[]{:S(2)}) async-start(), calls=%async_computation.18 | async-start | bytes 5980160 | tf_op jit(solution)/shard_map/reduce_scatter | solution.py:141
  230.6 35.3 %copy-start.27 = (bf16[128]{0:T(256)(128)(2,1)S(1)}, bf16[128]{0:T(256)(128)(2,1)}, u32[]{:S(2)}) copy-start(bf16[128]{0:T(256)(128)(2,1)} %param.24) | copy-start | bytes 772
  232.5 31.1 %copy-start.12 = (bf16[584,1024]{1,0:T(8,128)(2,1)}, bf16[584,1024]{1,0:T(8,128)(2,1)S(1)}, u32[]{:S(2)}) copy-start(bf16[584,1024]{1,0:T(8,128)(2,1)S(1)} %get-tuple-element.310) | copy-start | bytes 3588100
  232.5 13.9 %collective-permute-start = (bf16[584,1024]{1,0:T(8,128)(2,1)S(1)}, bf16[584,1024]{1,0:T(8,128)(2,1)S(1)}, u32[]{:S(2)}, u32[]{:S(2)}) collective-permute-start(bf16[584,1024]{1,0:T(8,128)(2,1)S(1)} %get-tuple-element.310), channel_id=1, source_target_pairs={{0,3},{1,0},{2,1},{3,2},{4,7},{5,4},{6,5},{7,6},{8,11},{9,8},{10,9... | collective-permute-start | bytes 3588104 | tf_op jit(solution)/shard_map/ppermute | solution.py:16
  247.4 16.2 %collective-permute-start.1 = (bf16[584,1024]{1,0:T(8,128)(2,1)S(1)}, bf16[584,1024]{1,0:T(8,128)(2,1)}, u32[]{:S(2)}, u32[]{:S(2)}) collective-permute-start(bf16[584,1024]{1,0:T(8,128)(2,1)S(1)} %collective-permute-done), channel_id=1, source_target_pairs={{0,3},{1,0},{2,1},{3,2},{4,7},{5,4},{6,5},{7,6},{8,11},{9,8},{10,9... | collective-permute-start | bytes 3588104 | tf_op jit(solution)/shard_map/ppermute | solution.py:16
  263.6 27.6 %collective-permute-start.2 = (bf16[584,1024]{1,0:T(8,128)(2,1)}, bf16[584,1024]{1,0:T(8,128)(2,1)}, u32[]{:S(2)}, u32[]{:S(2)}) collective-permute-start(bf16[584,1024]{1,0:T(8,128)(2,1)} %collective-permute-done.1), channel_id=1, source_target_pairs={{0,3},{1,0},{2,1},{3,2},{4,7},{5,4},{6,5},{7,6},{8,11},{9,8},{10,9... | collective-permute-start | bytes 3588104 | tf_op jit(solution)/shard_map/ppermute | solution.py:16
  288.7 5.0 copy-start.13
  366.8 14.8 %copy-start.28 = (bf16[1024,1024]{1,0:T(8,128)(2,1)S(1)}, bf16[1024,1024]{1,0:T(8,128)(2,1)}, u32[]{:S(2)}) copy-start(bf16[1024,1024]{1,0:T(8,128)(2,1)} %all-gather.13.cloned.1.call-done) | copy-start | bytes 6291460
  388.4 99.3 %reduce-scatter.26.cloned.1.call-start = ((), (), s32[]{:S(2)}) async-start(), calls=%async_computation.16 | async-start | bytes 5980160 | tf_op jit(solution)/shard_map/reduce_scatter | solution.py:124
  398.2 89.5 %copy-start.24 = (f32[1,1024]{1,0:T(1,128)S(1)}, f32[1,1024]{1,0:T(1,128)}, u32[]{:S(2)}) copy-start(f32[1,1024]{1,0:T(1,128)} %get-tuple-element.322) | copy-start | bytes 12292
  398.2 134.3 %all-gather.19.cloned.1.call-start = ((), (), s32[]{:S(2)}) async-start(), calls=%async_computation.19 | async-start | bytes 5980160 | tf_op jit(solution)/shard_map/all_gather | solution.py:147
  494.6 190.8 %reduce-scatter.44.cloned.1.call-start = ((), (), s32[]{:S(2)}) async-start(), calls=%async_computation.27 | async-start | bytes 2359296
  508.6 178.7 %reduce-scatter.32.cloned.1.call-start = ((), (), s32[]{:S(2)}) async-start(), calls=%async_computation.21 | async-start | bytes 2359296 | tf_op jit(solution)/shard_map/reduce_scatter | solution.py:213
  518.6 221.0 %reduce-scatter.40.cloned.1.call-start = ((), (), s32[]{:S(2)}) async-start(), calls=%async_computation.25 | async-start | bytes 73728
  617.6 7.2 copy-start.5
  624.7 180.3 %reduce-scatter.42.cloned.1.call-start = ((), (), s32[]{:S(2)}) async-start(), calls=%async_computation.26 | async-start | bytes 589824
  638.2 233.9 %reduce-scatter.38.cloned.1.call-start = ((), (), s32[]{:S(2)}) async-start(), calls=%async_computation.24 | async-start | bytes 1769472
  652.9 269.0 %reduce-scatter.30.cloned.1.call-start = ((), (), s32[]{:S(2)}) async-start(), calls=%async_computation.20 | async-start | bytes 5980160 | tf_op jit(solution)/shard_map/reduce_scatter | solution.py:188
  661.6 260.3 %copy-start.18 = (f32[584]{0:T(1024)S(1)}, f32[584]{0:T(1024)}, u32[]{:S(2)}) copy-start(f32[584]{0:T(1024)} %copy-done.17) | copy-start | bytes 7012
  661.6 260.3 %copy-start.20 = (f32[584]{0:T(1024)S(1)}, f32[584]{0:T(1024)}, u32[]{:S(2)}) copy-start(f32[584]{0:T(1024)} %copy-done.19) | copy-start | bytes 7012
  661.6 260.3 %copy-start.22 = (f32[1,1024]{1,0:T(1,128)S(1)}, f32[1,1024]{1,0:T(1,128)}, u32[]{:S(2)}) copy-start(f32[1,1024]{1,0:T(1,128)} %copy-done.21) | copy-start | bytes 12292
  661.6 398.1 %reduce-scatter.34.cloned.1.call-start = ((), (), s32[]{:S(2)}) async-start(), calls=%async_computation.22 | async-start | bytes 540672
  925.5 266.1 %reduce-scatter.36.cloned.1.call-start = ((), (), s32[]{:S(2)}) async-start(), calls=%async_computation.23 | async-start | bytes 540672
  (28 other events, 63.2 us)
Sparse Core Ops, SparseCore 0:
  10.2 46.6 all-gather.10
  59.1 36.6 all-gather.8
  179.3 46.1 reduce-scatter.23
  227.6 49.2 all-gather.12
  279.0 49.5 all-gather.14
  330.7 35.9 all-gather.16
  388.6 48.2 reduce-scatter.27
  439.4 48.2 reduce-scatter.25
  494.7 37.8 all-gather.18
  536.4 67.9 reduce-scatter.43
  608.3 66.8 reduce-scatter.31
  679.4 60.1 reduce-scatter.39
  743.9 60.9 reduce-scatter.41
  808.2 63.8 reduce-scatter.37
  874.7 47.1 reduce-scatter.29
  925.6 134.0 reduce-scatter.33
  1061.9 129.6 reduce-scatter.35
